TPU v7x, 32 devices: a whole 2x2x4 slice. The times are simulated.
32 devices in a mesh: tm: 16 (over z, y, core), rows: 2 (over x).
Axes of the slice: x: 2, y: 2, z: 4, core: 2. Of those that a mesh axis runs over, the one named last changes fastest.
Arguments:
- latents: bfloat16 [128, 4, 32, 512], P('tm', 'rows'), may hold values from -6 to 6
- clip_ids: int32 [128], replicated, may hold values from 0 to 24, never falling along the last dimension, each value on 1 to 9 neighbouring positions
- gain_in: float32 [512], replicated, may hold values from 0.25 to 1.75
- w_space: bfloat16 [3, 3, 512, 512], P(None, None, None, 'tm'), may hold values from -0.09375 to 0.09375
- w_time: bfloat16 [3, 512, 512], replicated, may hold values from -0.15625 to 0.15625
- gain_attn: float32 [512], replicated, may hold values from 0.25 to 1.75
- w_qkv: bfloat16 [512, 1536], replicated, may hold values from -0.25 to 0.25
- w_out: bfloat16 [512, 512], replicated, may hold values from -0.25 to 0.25
Outputs:
- block_out: bfloat16 [128, 4, 32, 512], P('tm', 'rows')
Inputs may be any that keep to these rules, and one draw needn't show every extreme that they name: `clip_ids`: clip numbers never fall along time; each clip has 1 to 9 frames and some clip has exactly 9.
All inputs are finite; a program needn't handle non-finite values.
Results may differ from a plain program's by a relative error of at most 0.0085.
Values may be sent and summed in bfloat16 or wider, within the bound.
No kernel may reach another device: no remote copies, remote signals or barrier semaphores. Data moves between devices by JAX's collectives and lax.ppermute only.
A program may use at most 64 MiB of HBM per device.

v0:
```python
import jax
import jax.numpy as jnp
from jax import lax
from jax.sharding import PartitionSpec as P


def with_halo(cells, sides, width):
    for axis, dim in sides:
        count = lax.axis_size(axis)
        ends = count - 1
        head = lax.slice_in_dim(cells, 0, width, axis=dim)
        tail = lax.slice_in_dim(cells, cells.shape[dim] - width, cells.shape[dim], axis=dim)
        cells = jnp.concatenate(
            [
                lax.ppermute(tail, axis, [(i, (i + 1) % count) for i in range(ends)]),
                cells,
                lax.ppermute(head, axis, [((i + 1) % count, i) for i in range(ends)]),
            ],
            axis=dim,
        )
    return cells


def shifted(array, axis, by):
    length = lax.axis_size(axis)
    pairs = [(i, i + by) for i in range(length) if 0 <= i + by < length]
    return lax.ppermute(array, axis, pairs)


def entering(array, axis, combine, identity):
    length, index = (lax.axis_size(axis), lax.axis_index(axis))
    everything = jax.tree.map(
        lambda part, kind: lax.all_gather(part.astype(kind), axis),
        array,
        (jnp.bfloat16, jnp.bfloat16, jnp.bfloat16),
    )
    start = jax.tree.map(
        lambda part, zero: jnp.broadcast_to(jnp.asarray(zero, part.dtype), part.shape),
        array,
        identity,
    )

    def step(k, before):
        reached = k < index
        new = combine(
            before, jax.tree.map(lambda part, own: part[k].astype(own.dtype), everything, array)
        )
        return jax.tree.map(lambda a, b: jnp.where(reached, a, b), new, before)

    return lax.fori_loop(0, length, step, start)


def rms_scale(values, gain):
    floats = values.astype(jnp.float32)
    scale = lax.rsqrt(jnp.mean(floats * floats, axis=-1, keepdims=True) + 1e-06)
    return (floats * scale * gain).astype(jnp.bfloat16)


def join_clip(earlier, later):
    early_sum, early_num, early_flag = earlier
    late_sum, late_num, late_flag = later
    pick = late_flag > 0
    return (
        jnp.where(pick, late_sum, early_sum + late_sum),
        jnp.where(pick, late_num, early_num + late_num),
        jnp.maximum(early_flag, late_flag),
    )


def attend_frames(tokens, chans):
    query = tokens[:, :, :chans]
    key = tokens[:, :, chans : 2 * chans]
    value = tokens[:, :, 2 * chans :]
    scores = jnp.einsum("fqc,fkc->fqk", query, key, preferred_element_type=jnp.float32) * chans ** (
        -0.5
    )
    probs = jax.nn.softmax(scores, axis=-1).astype(jnp.bfloat16)
    return jnp.einsum("fqk,fkc->fqc", probs, value, preferred_element_type=jnp.float32).astype(
        jnp.bfloat16
    )


def local(latents, clip_ids, gain_in, w_space, w_time, gain_attn, w_qkv, w_out):
    frames, height, width, chans = latents.shape
    groups = lax.axis_size("rows")
    normed = rms_scale(latents, gain_in)
    padded = with_halo(normed, (("rows", 1),), 1)
    padded = jnp.pad(padded, ((0, 0), (0, 0), (1, 1), (0, 0)))
    windows = [
        padded[:, dy : dy + height, dx : dx + width, :].reshape(-1, chans)
        for dy in range(3)
        for dx in range(3)
    ]
    piece = lax.all_gather(w_space, "tm", axis=3, tiled=True)
    total = jnp.zeros((windows[0].shape[0], piece.shape[3]), jnp.float32)
    for dy in range(3):
        for dx in range(3):
            total = total + jnp.dot(
                windows[dy * 3 + dx], piece[dy, dx], preferred_element_type=jnp.float32
            )
    conv = total
    acts = jax.nn.silu(conv).astype(jnp.bfloat16).reshape(frames, height, width, chans)
    earlier = shifted(acts[frames - 2 :], "tm", 1)
    extended = jnp.concatenate([earlier, acts], 0)
    first = lax.axis_index("tm") * frames
    seg_pad = jnp.concatenate([jnp.full((2,), -1, jnp.int32), clip_ids])
    seg_ext = lax.dynamic_slice_in_dim(seg_pad, first, frames + 2)
    segs = seg_ext[2:]
    total = latents.astype(jnp.float32).reshape(-1, chans)
    for back in range(3):
        source = extended[2 - back : 2 - back + frames]
        keep = (seg_ext[2 - back : 2 - back + frames] == segs).astype(jnp.bfloat16)[
            :, None, None, None
        ]
        total = total + jnp.dot(
            (source * keep).reshape(-1, chans), w_time[back], preferred_element_type=jnp.float32
        )
    resid = total.astype(jnp.bfloat16).reshape(frames, height, width, chans)
    floats = resid.astype(jnp.float32)
    sums_local = []
    nums_local = []
    running = floats[0]
    number = jnp.float32(1.0)
    sums_local.append(running)
    nums_local.append(number)
    for index in range(1, frames):
        same = segs[index] == segs[index - 1]
        running = jnp.where(same, running, jnp.float32(0.0)) + floats[index]
        number = jnp.where(same, number, jnp.float32(0.0)) + jnp.float32(1.0)
        sums_local.append(running)
        nums_local.append(number)
    last_num = jnp.reshape(number, (1,))
    flag = jnp.reshape((segs[frames - 1] != seg_ext[1]).astype(jnp.float32), (1,))
    empty = (jnp.zeros_like(running), jnp.zeros((1,), jnp.float32), jnp.zeros((1,), jnp.float32))
    carry_sum, carry_num, carry_flag = entering((running, last_num, flag), "tm", join_clip, empty)
    mixed_list = []
    for index in range(frames):
        cont = segs[index] == seg_ext[1]
        clip_sum = sums_local[index] + jnp.where(cont, carry_sum, jnp.float32(0.0))
        clip_num = nums_local[index] + jnp.where(cont, carry_num[0], jnp.float32(0.0))
        mixed_list.append((floats[index] + clip_sum / clip_num).astype(jnp.bfloat16))
    mixed = jnp.stack(mixed_list, 0)
    attn_in = rms_scale(mixed, gain_attn)
    qkv = jnp.dot(attn_in.reshape(-1, chans), w_qkv, preferred_element_type=jnp.float32).astype(
        jnp.bfloat16
    )
    grouped = qkv.reshape(groups, frames // groups, height, width, 3 * chans)
    block = lax.all_to_all(grouped, "rows", split_axis=0, concat_axis=2, tiled=True)
    count = block.shape[1]
    tokens = block.reshape(count, -1, 3 * chans)
    out = attend_frames(tokens, chans)
    attended = out.reshape(1, count, height * groups, width, chans)
    returned = lax.all_to_all(attended, "rows", split_axis=2, concat_axis=0, tiled=True)
    result = mixed.astype(jnp.float32).reshape(-1, chans) + jnp.dot(
        returned.reshape(-1, chans), w_out, preferred_element_type=jnp.float32
    )
    return result.astype(jnp.bfloat16).reshape(frames, height, width, chans)


def solution(mesh):
    placed = (P("tm", "rows", None, None), P(), P(), P(None, None, None, "tm"), P(), P(), P(), P())
    return jax.shard_map(
        local, mesh=mesh, in_specs=placed, out_specs=P("tm", "rows", None, None), check_vma=False
    )
```

profile of v0, /device:TPU:0, one launch (start us, length us, event | category | flops | bytes accessed | tf_op | source)
XLA Modules:
  0.0 244.3 jit_solution(15914931476498741329)
XLA Ops:
  9.9 4.9 %collective-permute-start = (bf16[8,1,32,512]{3,2,1,0:T(8,128)(2,1)S(1)}, bf16[8,1,32,512]{3,2,1,0:T(8,128)(2,1)S(1)}, u32[]{:S(2)}, u32[]{:S(2)}) collective-permute-start(bf16[8,1,32,512]{3,2,1,0:T(8,128)(2,1)S(1)} %get-tuple-element.195), channel_id=1, source_target_pairs={{0,1},{2,3},{4,5},{6,7},{8,9},{10,11},{12,13},{14,15},{16,17},{18,... | collective-permute-start | bytes 786440 | tf_op jit(solution)/shard_map/ppermute | solution.py:15
  27.5 1.7 fusion.34
  29.2 36.5 %all-gather.4.cloned.1.call-done = bf16[3,3,512,512]{2,3,1,0:T(8,128)(2,1)} async-done(((bf16[3,3,512,32]{2,3,1,0:T(8,128)(2,1)}), bf16[3,3,512,512]{2,3,1,0:T(8,128)(2,1)}) %all-gather.4.cloned.1.call-update) | async-done | bytes 4718608 | tf_op jit(solution)/shard_map/all_gather | solution.py:94
  65.7 1.8 fusion.23
  67.5 1.7 fusion.22
  69.2 1.6 convolution_add_fusion.10
  74.9 2.2 collective-permute-start.2
  83.2 31.5 %all-reduce.4 = (bf16[16]{0:T(256)(128)(2,1)S(1)}, bf16[16]{0:T(256)(128)(2,1)S(1)}) all-reduce(bf16[16]{0:T(256)(128)(2,1)S(1)} %dynamic-update-slice, bf16[16]{0:T(256)(128)(2,1)S(1)} %dynamic-update-slice.1), channel_id=2, replica_groups=mesh['tm'=16,'rows'=2] {'tm'}, use_global_device_ids=true, to_apply=%add.2 | all-reduce | flops 32 | bytes 128
  125.0 75.8 %while.16 = (s32[]{:T(128)}, f32[2,32,512]{2,1,0:T(8,128)S(1)}, f32[1]{0:T(128)}, s32[]{:T(128)}, bf16[16,1]{0,1:T(2,128)(2,1)S(1)}, /*index=5*/bf16[16,2,32,512...) while((s32[]{:T(128)}, f32[2,32,512]{2,1,0:T(8,128)S(1)}, f32[1]{0:T(128)}, ...), condition=%wide.region_2.3_spmd.clone, body=%wide.region_1.2_spmd.clone.sunk | while | flops 163849 | bytes 327847 | solution.py:50
  128.2 1.5 fusion.61
  133.0 1.5 fusion.61
  137.7 1.5 fusion.61
  142.4 1.5 fusion.61
  147.2 1.5 fusion.61
  151.9 1.5 fusion.61
  156.6 1.5 fusion.61
  161.4 1.5 fusion.61
  166.1 1.5 fusion.61
  170.9 1.5 fusion.61
  175.6 1.5 fusion.61
  180.3 1.5 fusion.61
  199.3 1.5 fusion.61
  203.0 20.9 %all_to_all.30 = bf16[2,4,2,32,1536]{4,3,2,1,0:T(8,128)(2,1)S(1)} all-to-all(bf16[2,4,2,32,1536]{4,3,2,1,0:T(8,128)(2,1)S(1)} %bitcast.174), channel_id=1, replica_groups=mesh['tm'=16,'rows'=2] {'rows'}, dimensions={0} | all-to-all | bytes 3145728 | tf_op jit(solution)/shard_map/all_to_all | solution.py:148
  227.1 9.1 %all_to_all.31 = bf16[1,4,4,32,512]{4,3,1,0,2:T(8,128)(2,1)S(1)} all-to-all(bf16[1,4,4,32,512]{4,3,1,0,2:T(8,128)(2,1)S(1)} %copy.18), channel_id=1, replica_groups=mesh['tm'=16,'rows'=2] {'rows'}, dimensions={2} | all-to-all | bytes 1048576 | tf_op jit(solution)/shard_map/all_to_all | solution.py:153
  (126 shorter events, 49.3 us)
Async XLA Ops:
  6.5 195.4 %copy-start = (bf16[512,1536]{1,0:T(8,128)(2,1)S(1)}, bf16[512,1536]{1,0:T(8,128)(2,1)}, u32[]{:S(2)}) copy-start(bf16[512,1536]{1,0:T(8,128)(2,1)} %param.16) | copy-start | bytes 4718596
  6.5 9.5 %copy-start.14 = (s32[128]{0:T(128)S(1)}, s32[128]{0:T(128)}, u32[]{:S(2)}) copy-start(s32[128]{0:T(128)} %param.11) | copy-start | bytes 1540
  6.5 59.2 %all-gather.4.cloned.1.call-start = ((), (), s32[]{:S(2)}) async-start(), calls=%async_computation.2 | async-start | bytes 5013504 | tf_op jit(solution)/shard_map/all_gather | solution.py:94
  7.3 117.8 %all-gather.6.cloned.1.call-start = ((), (), s32[]{:S(2)}) async-start(), calls=%async_computation.3 | async-start | bytes 1114112 | tf_op jit(solution)/shard_map/all_gather | solution.py:33
  9.9 15.8 %collective-permute-start = (bf16[8,1,32,512]{3,2,1,0:T(8,128)(2,1)S(1)}, bf16[8,1,32,512]{3,2,1,0:T(8,128)(2,1)S(1)}, u32[]{:S(2)}, u32[]{:S(2)}) collective-permute-start(bf16[8,1,32,512]{3,2,1,0:T(8,128)(2,1)S(1)} %get-tuple-element.195), channel_id=1, source_target_pairs={{0,1},{2,3},{4,5},{6,7},{8,9},{10,11},{12,13},{14,15},{16,17},{18,... | collective-permute-start | bytes 786440 | tf_op jit(solution)/shard_map/ppermute | solution.py:15
  14.7 11.0 %collective-permute-start.1 = (bf16[8,1,32,512]{3,2,1,0:T(8,128)(2,1)S(1)}, bf16[8,1,32,512]{3,2,1,0:T(8,128)(2,1)S(1)}, u32[]{:S(2)}, u32[]{:S(2)}) collective-permute-start(bf16[8,1,32,512]{3,2,1,0:T(8,128)(2,1)S(1)} %get-tuple-element.196), channel_id=1, source_target_pairs={{1,0},{3,2},{5,4},{7,6},{9,8},{11,10},{13,12},{15,14},{17,16},{19,... | collective-permute-start | bytes 786440 | tf_op jit(solution)/shard_map/ppermute | solution.py:17
  65.7 1.8 copy-start.5
  65.7 3.4 %copy-start.6 = (bf16[8,2,32,512]{3,2,1,0:T(8,128)(2,1)S(1)}, bf16[8,2,32,512]{3,2,1,0:T(8,128)(2,1)}, u32[]{:S(2)}) copy-start(bf16[8,2,32,512]{3,2,1,0:T(8,128)(2,1)} %get-tuple-element.194) | copy-start | bytes 1572868
  67.5 3.3 %copy-start.2 = (bf16[3,3,512,512]{2,3,1,0:T(8,128)(2,1)S(1)}, bf16[3,3,512,512]{2,3,1,0:T(8,128)(2,1)}, u32[]{:S(2)}) copy-start(bf16[3,3,512,512]{2,3,1,0:T(8,128)(2,1)} %all-gather.4.cloned.1.call-done) | copy-start | bytes 14155780
  69.1 1.6 copy-start.4
  70.7 1.0 copy-start.3
  73.2 1.0 copy-start.10
  74.3 2.8 %copy-start.1 = (bf16[8,2,32,512]{3,2,1,0:T(8,128)(2,1)S(1)}, bf16[8,2,32,512]{3,2,1,0:T(8,128)(2,1)}, u32[]{:S(2)}) copy-start(bf16[8,2,32,512]{3,2,1,0:T(8,128)(2,1)} %param.10) | copy-start | bytes 1572868
  74.3 2.8 %copy-start.8 = (bf16[3,512,512]{2,1,0:T(8,128)(2,1)S(1)}, bf16[3,512,512]{2,1,0:T(8,128)(2,1)}, u32[]{:S(2)}) copy-start(bf16[3,512,512]{2,1,0:T(8,128)(2,1)} %param.14) | copy-start | bytes 4718596
  74.9 3.1 %collective-permute-start.2 = (bf16[2,2,32,512]{3,2,1,0:T(8,128)(2,1)S(1)}, bf16[2,2,32,512]{3,2,1,0:T(8,128)(2,1)S(1)}, u32[]{:S(2)}, u32[]{:S(2)}) collective-permute-start(bf16[2,2,32,512]{3,2,1,0:T(8,128)(2,1)S(1)} %bitcast.187), channel_id=1, source_target_pairs={{0,2},{2,4},{4,6},{6,8},{8,10},{10,12},{12,14},{14,16},{16,18},{18... | collective-permute-start | bytes 393224 | tf_op jit(solution)/shard_map/ppermute | solution.py:27
  79.1 1.4 copy-start.15
  125.0 76.0 %copy-start.12 = (f32[64,512]{1,0:T(8,128)S(1)}, f32[64,512]{1,0:T(8,128)}, u32[]{:S(2)}) copy-start(f32[64,512]{1,0:T(8,128)} %get-tuple-element.188) | copy-start | bytes 393220
  125.0 76.1 %copy-start.11 = (f32[64,512]{1,0:T(8,128)S(1)}, f32[64,512]{1,0:T(8,128)}, u32[]{:S(2)}) copy-start(f32[64,512]{1,0:T(8,128)} %get-tuple-element.186) | copy-start | bytes 393220
  201.1 0.7 copy-start.13
  224.0 1.2 copy-start.7
  227.0 9.2 %copy-start.9 = (bf16[512,512]{1,0:T(8,128)(2,1)S(1)}, bf16[512,512]{1,0:T(8,128)(2,1)}, u32[]{:S(2)}) copy-start(bf16[512,512]{1,0:T(8,128)(2,1)} %param.17) | copy-start | bytes 1572868
Sparse Core Ops, SparseCore 0:
  9.5 56.0 all-gather.3
  80.0 40.4 all-gather.5
where the time goes:
time: 246 us; the launch traced here: 244 us
  blocking collectives  61.5 us (25%)
  other arithmetic  41.5 us (17%)
  waiting for transfers between devices  37.7 us (15%)
  between operations  32.4 us (13%)
  loops' own time  31.1 us (13%)
  local copies, waits for them, and re-layouts  18.6 us (8%)
  matrix products  13.2 us (5%)
  starting transfers between devices  8.35 us (3%)
    all_gather x1, waiting for transfers between devices, local(): piece = lax.all_gather(w_space, 'tm', axis=3, tiled=True)  36.5 us
    unnamed x1, blocking collectives  31.5 us
    another operation x1, loops' own time, entering(): return lax.fori_loop(0, length, step, start)  31.1 us
    select_n x16, other arithmetic, step(): return jax.tree.map(lambda a, b: jnp.where(reached, a, b), new, before)  24.5 us
    all_to_all x1, blocking collectives, local(): lax.all_to_all(grouped, 'rows', split_axis=0, concat_axis=2, tiled=True)  20.9 us
    gt x16, other arithmetic, join_clip(): pick = late_flag > 0  10.4 us
    dynamic_slice x16, local copies, waits for them, and re-layouts, step(): part[k].astype(own.dtype)  9.82 us
    all_to_all x1, blocking collectives, local(): lax.all_to_all(attended, 'rows', split_axis=2, concat_axis=0, tiled=True)  9.12 us
  transfers between devices with their start and end apart: 5, of which 2 were waited for; matrix products, arithmetic and copies ran while one was open for 5% of the time, Pallas kernels for 0%

commit v1 on v0

--- a/solution.py
+++ b/solution.py
@@ -2,6 +2,22 @@
 import jax.numpy as jnp
 from jax import lax
 from jax.sharding import PartitionSpec as P
+
+
+def gather_around(x, axis, dim):
+    ways, here, step = (lax.axis_size(axis), lax.axis_index(axis), x.shape[dim])
+    shape = [n * ways if d == dim else n for d, n in enumerate(x.shape)]
+    full = lax.dynamic_update_slice_in_dim(jnp.zeros(shape, x.dtype), x, here * step, axis=dim)
+    going_up = going_down = x
+    for far in range(1, ways // 2 + 1):
+        going_up = lax.ppermute(going_up, axis, [(d, (d + 1) % ways) for d in range(ways)])
+        full = lax.dynamic_update_slice_in_dim(full, going_up, (here - far) % ways * step, axis=dim)
+        if 2 * far < ways:
+            going_down = lax.ppermute(going_down, axis, [(d, (d - 1) % ways) for d in range(ways)])
+            full = lax.dynamic_update_slice_in_dim(
+                full, going_down, (here + far) % ways * step, axis=dim
+            )
+    return full
 
 
 def with_halo(cells, sides, width):
@@ -91,7 +107,7 @@
         for dy in range(3)
         for dx in range(3)
     ]
-    piece = lax.all_gather(w_space, "tm", axis=3, tiled=True)
+    piece = gather_around(w_space, "tm", 3)
     total = jnp.zeros((windows[0].shape[0], piece.shape[3]), jnp.float32)
     for dy in range(3):
         for dx in range(3):

time: 246 us -> 272 us (1.11)
  starting transfers between devices: 8.35 us -> 39 us
  waiting for transfers between devices: 37.7 us -> 33.4 us
  matrix products: 13.2 us -> 9.95 us
    all_gather x1 -> x0, waiting for transfers between devices: 36.5 us -> none  [local(): piece = lax.all_gather(w_space, 'tm', axis=3, tiled=True)]
    ppermute x0 -> x15, waiting for transfers between devices: none -> 32.9 us  [the longest x8 32.9 us: gather_around(): lax.ppermute(going_up, axis, [(d, (d + 1) % ways) for d in range(ways)])]
    ppermute x0 -> x15, starting transfers between devices: none -> 32.6 us  [the longest x7 32.1 us: gather_around(): lax.ppermute(going_down, axis, [(d, (d - 1) % ways) for d in range(ways)])]
    dot_general x9, matrix products: 7.94 us -> 4.71 us  [local(): jnp.dot(windows[dy * 3 + dx], piece[dy, dx], preferred_element_type=jnp.f...]
  transfers between devices with their start and end apart: 5 -> 19, of which waited for: 2 -> 8; matrix products, arithmetic and copies ran while one was open for 5% -> 4% of each run, Pallas kernels for 0% -> 0%
where the time goes in v1:
time: 272 us; the launch traced here: 270 us
  blocking collectives  61.6 us (23%)
  other arithmetic  43.4 us (16%)
  starting transfers between devices  39 us (14%)
  waiting for transfers between devices  33.4 us (12%)
  between operations  32.5 us (12%)
  loops' own time  31 us (11%)
  local copies, waits for them, and re-layouts  18.7 us (7%)
  matrix products  9.95 us (4%)
    ppermute x8, waiting for transfers between devices, gather_around(): lax.ppermute(going_up, axis, [(d, (d + 1) % ways) for d in range(ways)])  32.9 us
    ppermute x7, starting transfers between devices, gather_around(): lax.ppermute(going_down, axis, [(d, (d - 1) % ways) for d in range(ways)])  32.1 us
    another operation x1, loops' own time, entering(): return lax.fori_loop(0, length, step, start)  31 us
    unnamed x1, blocking collectives  30.1 us
    select_n x16, other arithmetic, step(): return jax.tree.map(lambda a, b: jnp.where(reached, a, b), new, before)  25.4 us
    all_to_all x1, blocking collectives, local(): lax.all_to_all(grouped, 'rows', split_axis=0, concat_axis=2, tiled=True)  22.5 us
    gt x16, other arithmetic, join_clip(): pick = late_flag > 0  10.5 us
    dynamic_slice x16, local copies, waits for them, and re-layouts, step(): part[k].astype(own.dtype)  9.82 us
  transfers between devices with their start and end apart: 19, of which 8 were waited for; matrix products, arithmetic and copies ran while one was open for 4% of the time, Pallas kernels for 0%

profile of v1, /device:TPU:0, one launch (start us, length us, event | category | flops | bytes accessed | tf_op | source)
XLA Modules:
  0.0 269.6 jit_solution(15903288565561301001)
XLA Ops:
  7.0 5.1 %collective-permute-start.3 = (bf16[3,3,512,32]{2,3,1,0:T(8,128)(2,1)}, bf16[3,3,512,32]{2,3,1,0:T(8,128)(2,1)S(1)}, u32[]{:S(2)}, u32[]{:S(2)}) collective-permute-start(bf16[3,3,512,32]{2,3,1,0:T(8,128)(2,1)} %param.13), channel_id=1, source_target_pairs={{0,30},{2,0},{4,2},{6,4},{8,6},{10,8},{12,10},{14,12},{16,14},{18,... | collective-permute-start | bytes 884744 | tf_op jit(solution)/shard_map/ppermute | solution.py:16
  15.4 3.8 %collective-permute-start = (bf16[8,1,32,512]{3,2,1,0:T(8,128)(2,1)}, bf16[8,1,32,512]{3,2,1,0:T(8,128)(2,1)S(1)}, u32[]{:S(2)}, u32[]{:S(2)}) collective-permute-start(bf16[8,1,32,512]{3,2,1,0:T(8,128)(2,1)} %get-tuple-element.195), channel_id=1, source_target_pairs={{0,1},{2,3},{4,5},{6,7},{8,9},{10,11},{12,13},{14,15},{16,17},{18,... | collective-permute-start | bytes 786440 | tf_op jit(solution)/shard_map/ppermute | solution.py:31
  31.1 4.4 %collective-permute-start.5 = (bf16[3,3,512,32]{2,3,1,0:T(8,128)(2,1)S(1)}, bf16[3,3,512,32]{2,3,1,0:T(8,128)(2,1)S(1)}, u32[]{:S(2)}, u32[]{:S(2)}) collective-permute-start(bf16[3,3,512,32]{2,3,1,0:T(8,128)(2,1)S(1)} %collective-permute-done.3), channel_id=1, source_target_pairs={{0,30},{2,0},{4,2},{6,4},{8,6},{10,8},{12,10},{14,12},{16,14},{18,... | collective-permute-start | bytes 884744 | tf_op jit(solution)/shard_map/ppermute | solution.py:16
  36.7 3.3 %collective-permute-done.4 = bf16[3,3,512,32]{2,3,1,0:T(8,128)(2,1)S(1)} collective-permute-done((bf16[3,3,512,32]{2,3,1,0:T(8,128)(2,1)S(1)}, bf16[3,3,512,32]{2,3,1,0:T(8,128)(2,1)S(1)}, u32[]{:S(2)}, u32[]{:S(2)}) %collective-permute-start.4) | collective-permute-done | bytes 294944 | tf_op jit(solution)/shard_map/ppermute | solution.py:13
  40.0 4.5 %collective-permute-start.7 = (bf16[3,3,512,32]{2,3,1,0:T(8,128)(2,1)S(1)}, bf16[3,3,512,32]{2,3,1,0:T(8,128)(2,1)S(1)}, u32[]{:S(2)}, u32[]{:S(2)}) collective-permute-start(bf16[3,3,512,32]{2,3,1,0:T(8,128)(2,1)S(1)} %collective-permute-done.5), channel_id=1, source_target_pairs={{0,30},{2,0},{4,2},{6,4},{8,6},{10,8},{12,10},{14,12},{16,14},{18,... | collective-permute-start | bytes 884744 | tf_op jit(solution)/shard_map/ppermute | solution.py:16
  45.1 3.8 %collective-permute-done.6 = bf16[3,3,512,32]{2,3,1,0:T(8,128)(2,1)S(1)} collective-permute-done((bf16[3,3,512,32]{2,3,1,0:T(8,128)(2,1)S(1)}, bf16[3,3,512,32]{2,3,1,0:T(8,128)(2,1)S(1)}, u32[]{:S(2)}, u32[]{:S(2)}) %collective-permute-start.6) | collective-permute-done | bytes 294944 | tf_op jit(solution)/shard_map/ppermute | solution.py:13
  49.1 4.5 %collective-permute-start.9 = (bf16[3,3,512,32]{2,3,1,0:T(8,128)(2,1)S(1)}, bf16[3,3,512,32]{2,3,1,0:T(8,128)(2,1)S(1)}, u32[]{:S(2)}, u32[]{:S(2)}) collective-permute-start(bf16[3,3,512,32]{2,3,1,0:T(8,128)(2,1)S(1)} %collective-permute-done.7), channel_id=1, source_target_pairs={{0,30},{2,0},{4,2},{6,4},{8,6},{10,8},{12,10},{14,12},{16,14},{18,... | collective-permute-start | bytes 884744 | tf_op jit(solution)/shard_map/ppermute | solution.py:16
  53.6 4.3 %collective-permute-done.8 = bf16[3,3,512,32]{2,3,1,0:T(8,128)(2,1)S(1)} collective-permute-done((bf16[3,3,512,32]{2,3,1,0:T(8,128)(2,1)S(1)}, bf16[3,3,512,32]{2,3,1,0:T(8,128)(2,1)S(1)}, u32[]{:S(2)}, u32[]{:S(2)}) %collective-permute-start.8) | collective-permute-done | bytes 294944 | tf_op jit(solution)/shard_map/ppermute | solution.py:13
  58.0 4.6 %collective-permute-start.11 = (bf16[3,3,512,32]{2,3,1,0:T(8,128)(2,1)S(1)}, bf16[3,3,512,32]{2,3,1,0:T(8,128)(2,1)S(1)}, u32[]{:S(2)}, u32[]{:S(2)}) collective-permute-start(bf16[3,3,512,32]{2,3,1,0:T(8,128)(2,1)S(1)} %collective-permute-done.9), channel_id=1, source_target_pairs={{0,30},{2,0},{4,2},{6,4},{8,6},{10,8},{12,10},{14,12},{16,14},{18,... | collective-permute-start | bytes 884744 | tf_op jit(solution)/shard_map/ppermute | solution.py:16
  62.6 4.3 %collective-permute-done.10 = bf16[3,3,512,32]{2,3,1,0:T(8,128)(2,1)S(1)} collective-permute-done((bf16[3,3,512,32]{2,3,1,0:T(8,128)(2,1)S(1)}, bf16[3,3,512,32]{2,3,1,0:T(8,128)(2,1)S(1)}, u32[]{:S(2)}, u32[]{:S(2)}) %collective-permute-start.10) | collective-permute-done | bytes 294944 | tf_op jit(solution)/shard_map/ppermute | solution.py:13
  66.9 4.6 %collective-permute-start.13 = (bf16[3,3,512,32]{2,3,1,0:T(8,128)(2,1)S(1)}, bf16[3,3,512,32]{2,3,1,0:T(8,128)(2,1)S(1)}, u32[]{:S(2)}, u32[]{:S(2)}) collective-permute-start(bf16[3,3,512,32]{2,3,1,0:T(8,128)(2,1)S(1)} %collective-permute-done.11), channel_id=1, source_target_pairs={{0,30},{2,0},{4,2},{6,4},{8,6},{10,8},{12,10},{14,12},{16,14},{18,... | collective-permute-start | bytes 884744 | tf_op jit(solution)/shard_map/ppermute | solution.py:16
  71.5 4.3 %collective-permute-done.12 = bf16[3,3,512,32]{2,3,1,0:T(8,128)(2,1)S(1)} collective-permute-done((bf16[3,3,512,32]{2,3,1,0:T(8,128)(2,1)S(1)}, bf16[3,3,512,32]{2,3,1,0:T(8,128)(2,1)S(1)}, u32[]{:S(2)}, u32[]{:S(2)}) %collective-permute-start.12) | collective-permute-done | bytes 294944 | tf_op jit(solution)/shard_map/ppermute | solution.py:13
  75.9 4.6 %collective-permute-start.15 = (bf16[3,3,512,32]{2,3,1,0:T(8,128)(2,1)S(1)}, bf16[3,3,512,32]{2,3,1,0:T(8,128)(2,1)S(1)}, u32[]{:S(2)}, u32[]{:S(2)}) collective-permute-start(bf16[3,3,512,32]{2,3,1,0:T(8,128)(2,1)S(1)} %collective-permute-done.13), channel_id=1, source_target_pairs={{0,30},{2,0},{4,2},{6,4},{8,6},{10,8},{12,10},{14,12},{16,14},{18,... | collective-permute-start | bytes 884744 | tf_op jit(solution)/shard_map/ppermute | solution.py:16
  80.5 4.2 %collective-permute-done.14 = bf16[3,3,512,32]{2,3,1,0:T(8,128)(2,1)S(1)} collective-permute-done((bf16[3,3,512,32]{2,3,1,0:T(8,128)(2,1)S(1)}, bf16[3,3,512,32]{2,3,1,0:T(8,128)(2,1)S(1)}, u32[]{:S(2)}, u32[]{:S(2)}) %collective-permute-start.14) | collective-permute-done | bytes 294944 | tf_op jit(solution)/shard_map/ppermute | solution.py:13
  84.8 8.7 %collective-permute-done.16 = bf16[3,3,512,32]{2,3,1,0:T(8,128)(2,1)S(1)} collective-permute-done((bf16[3,3,512,32]{2,3,1,0:T(8,128)(2,1)S(1)}, bf16[3,3,512,32]{2,3,1,0:T(8,128)(2,1)S(1)}, u32[]{:S(2)}, u32[]{:S(2)}) %collective-permute-start.16) | collective-permute-done | bytes 294944 | tf_op jit(solution)/shard_map/ppermute | solution.py:13
  105.9 30.1 %all-reduce.4 = (bf16[16]{0:T(256)(128)(2,1)S(1)}, bf16[16]{0:T(256)(128)(2,1)S(1)}) all-reduce(bf16[16]{0:T(256)(128)(2,1)S(1)} %dynamic-update-slice, bf16[16]{0:T(256)(128)(2,1)S(1)} %dynamic-update-slice.1), channel_id=2, replica_groups=mesh['tm'=16,'rows'=2] {'tm'}, use_global_device_ids=true, to_apply=%add.2 | all-reduce | flops 32 | bytes 128
  146.2 76.8 %while.16 = (s32[]{:T(128)}, f32[2,32,512]{2,1,0:T(8,128)S(1)}, f32[1]{0:T(128)}, s32[]{:T(128)}, bf16[16,1]{0,1:T(2,128)(2,1)S(1)}, /*index=5*/bf16[16,2,32,512...) while((s32[]{:T(128)}, f32[2,32,512]{2,1,0:T(8,128)S(1)}, f32[1]{0:T(128)}, ...), condition=%wide.region_2.3_spmd.clone, body=%wide.region_1.2_spmd.clone.sunk | while | flops 163849 | bytes 327847 | solution.py:66
  149.4 1.6 fusion.73
  154.2 1.6 fusion.73
  159.0 1.6 fusion.73
  163.8 1.6 fusion.73
  168.6 1.6 fusion.73
  226.8 22.5 %all_to_all.30 = bf16[2,4,2,32,1536]{4,3,2,1,0:T(8,128)(2,1)S(1)} all-to-all(bf16[2,4,2,32,1536]{4,3,2,1,0:T(8,128)(2,1)S(1)} %bitcast.175), channel_id=1, replica_groups=mesh['tm'=16,'rows'=2] {'rows'}, dimensions={0} | all-to-all | bytes 3145728 | tf_op jit(solution)/shard_map/all_to_all | solution.py:164
  252.4 9.1 %all_to_all.31 = bf16[1,4,4,32,512]{4,3,1,0,2:T(8,128)(2,1)S(1)} all-to-all(bf16[1,4,4,32,512]{4,3,1,0,2:T(8,128)(2,1)S(1)} %copy.18), channel_id=1, replica_groups=mesh['tm'=16,'rows'=2] {'rows'}, dimensions={2} | all-to-all | bytes 1048576 | tf_op jit(solution)/shard_map/all_to_all | solution.py:169
  (154 shorter events, 67.7 us)
Async XLA Ops:
  6.5 219.2 %copy-start = (bf16[512,1536]{1,0:T(8,128)(2,1)S(1)}, bf16[512,1536]{1,0:T(8,128)(2,1)}, u32[]{:S(2)}) copy-start(bf16[512,1536]{1,0:T(8,128)(2,1)} %param.16) | copy-start | bytes 4718596
  6.5 29.4 %copy-start.5 = (bf16[3,3,512,32]{2,3,1,0:T(8,128)(2,1)S(1)}, bf16[3,3,512,32]{2,3,1,0:T(8,128)(2,1)}, u32[]{:S(2)}) copy-start(bf16[3,3,512,32]{2,3,1,0:T(8,128)(2,1)} %param.13) | copy-start | bytes 884740
  6.5 139.6 %all-gather.3.cloned.1.call-start = ((), (), s32[]{:S(2)}) async-start(), calls=%async_computation.2 | async-start | bytes 1114112 | tf_op jit(solution)/shard_map/all_gather | solution.py:49
  6.5 24.5 %collective-permute-start.2 = (bf16[3,3,512,32]{2,3,1,0:T(8,128)(2,1)}, bf16[3,3,512,32]{2,3,1,0:T(8,128)(2,1)S(1)}, u32[]{:S(2)}, u32[]{:S(2)}) collective-permute-start(bf16[3,3,512,32]{2,3,1,0:T(8,128)(2,1)} %param.13), channel_id=1, source_target_pairs={{0,2},{2,4},{4,6},{6,8},{8,10},{10,12},{12,14},{14,16},{16,18},{18... | collective-permute-start | bytes 884744 | tf_op jit(solution)/shard_map/ppermute | solution.py:13
  7.0 24.1 %collective-permute-start.3 = (bf16[3,3,512,32]{2,3,1,0:T(8,128)(2,1)}, bf16[3,3,512,32]{2,3,1,0:T(8,128)(2,1)S(1)}, u32[]{:S(2)}, u32[]{:S(2)}) collective-permute-start(bf16[3,3,512,32]{2,3,1,0:T(8,128)(2,1)} %param.13), channel_id=1, source_target_pairs={{0,30},{2,0},{4,2},{6,4},{8,6},{10,8},{12,10},{14,12},{16,14},{18,... | collective-permute-start | bytes 884744 | tf_op jit(solution)/shard_map/ppermute | solution.py:16
  15.4 20.6 %collective-permute-start = (bf16[8,1,32,512]{3,2,1,0:T(8,128)(2,1)}, bf16[8,1,32,512]{3,2,1,0:T(8,128)(2,1)S(1)}, u32[]{:S(2)}, u32[]{:S(2)}) collective-permute-start(bf16[8,1,32,512]{3,2,1,0:T(8,128)(2,1)} %get-tuple-element.195), channel_id=1, source_target_pairs={{0,1},{2,3},{4,5},{6,7},{8,9},{10,11},{12,13},{14,15},{16,17},{18,... | collective-permute-start | bytes 786440 | tf_op jit(solution)/shard_map/ppermute | solution.py:31
  19.2 16.8 %collective-permute-start.1 = (bf16[8,1,32,512]{3,2,1,0:T(8,128)(2,1)}, bf16[8,1,32,512]{3,2,1,0:T(8,128)(2,1)S(1)}, u32[]{:S(2)}, u32[]{:S(2)}) collective-permute-start(bf16[8,1,32,512]{3,2,1,0:T(8,128)(2,1)} %get-tuple-element.196), channel_id=1, source_target_pairs={{1,0},{3,2},{5,4},{7,6},{9,8},{11,10},{13,12},{15,14},{17,16},{19,... | collective-permute-start | bytes 786440 | tf_op jit(solution)/shard_map/ppermute | solution.py:33
  31.1 8.9 %collective-permute-start.4 = (bf16[3,3,512,32]{2,3,1,0:T(8,128)(2,1)S(1)}, bf16[3,3,512,32]{2,3,1,0:T(8,128)(2,1)S(1)}, u32[]{:S(2)}, u32[]{:S(2)}) collective-permute-start(bf16[3,3,512,32]{2,3,1,0:T(8,128)(2,1)S(1)} %collective-permute-done.2), channel_id=1, source_target_pairs={{0,2},{2,4},{4,6},{6,8},{8,10},{10,12},{12,14},{14,16},{16,18},{18... | collective-permute-start | bytes 884744 | tf_op jit(solution)/shard_map/ppermute | solution.py:13
  31.1 8.9 %collective-permute-start.5 = (bf16[3,3,512,32]{2,3,1,0:T(8,128)(2,1)S(1)}, bf16[3,3,512,32]{2,3,1,0:T(8,128)(2,1)S(1)}, u32[]{:S(2)}, u32[]{:S(2)}) collective-permute-start(bf16[3,3,512,32]{2,3,1,0:T(8,128)(2,1)S(1)} %collective-permute-done.3), channel_id=1, source_target_pairs={{0,30},{2,0},{4,2},{6,4},{8,6},{10,8},{12,10},{14,12},{16,14},{18,... | collective-permute-start | bytes 884744 | tf_op jit(solution)/shard_map/ppermute | solution.py:16
  40.0 8.9 %collective-permute-start.6 = (bf16[3,3,512,32]{2,3,1,0:T(8,128)(2,1)S(1)}, bf16[3,3,512,32]{2,3,1,0:T(8,128)(2,1)S(1)}, u32[]{:S(2)}, u32[]{:S(2)}) collective-permute-start(bf16[3,3,512,32]{2,3,1,0:T(8,128)(2,1)S(1)} %collective-permute-done.4), channel_id=1, source_target_pairs={{0,2},{2,4},{4,6},{6,8},{8,10},{10,12},{12,14},{14,16},{16,18},{18... | collective-permute-start | bytes 884744 | tf_op jit(solution)/shard_map/ppermute | solution.py:13
  40.0 9.1 %collective-permute-start.7 = (bf16[3,3,512,32]{2,3,1,0:T(8,128)(2,1)S(1)}, bf16[3,3,512,32]{2,3,1,0:T(8,128)(2,1)S(1)}, u32[]{:S(2)}, u32[]{:S(2)}) collective-permute-start(bf16[3,3,512,32]{2,3,1,0:T(8,128)(2,1)S(1)} %collective-permute-done.5), channel_id=1, source_target_pairs={{0,30},{2,0},{4,2},{6,4},{8,6},{10,8},{12,10},{14,12},{16,14},{18,... | collective-permute-start | bytes 884744 | tf_op jit(solution)/shard_map/ppermute | solution.py:16
  48.9 8.9 %collective-permute-start.8 = (bf16[3,3,512,32]{2,3,1,0:T(8,128)(2,1)S(1)}, bf16[3,3,512,32]{2,3,1,0:T(8,128)(2,1)S(1)}, u32[]{:S(2)}, u32[]{:S(2)}) collective-permute-start(bf16[3,3,512,32]{2,3,1,0:T(8,128)(2,1)S(1)} %collective-permute-done.6), channel_id=1, source_target_pairs={{0,2},{2,4},{4,6},{6,8},{8,10},{10,12},{12,14},{14,16},{16,18},{18... | collective-permute-start | bytes 884744 | tf_op jit(solution)/shard_map/ppermute | solution.py:13
  49.1 8.9 %collective-permute-start.9 = (bf16[3,3,512,32]{2,3,1,0:T(8,128)(2,1)S(1)}, bf16[3,3,512,32]{2,3,1,0:T(8,128)(2,1)S(1)}, u32[]{:S(2)}, u32[]{:S(2)}) collective-permute-start(bf16[3,3,512,32]{2,3,1,0:T(8,128)(2,1)S(1)} %collective-permute-done.7), channel_id=1, source_target_pairs={{0,30},{2,0},{4,2},{6,4},{8,6},{10,8},{12,10},{14,12},{16,14},{18,... | collective-permute-start | bytes 884744 | tf_op jit(solution)/shard_map/ppermute | solution.py:16
  57.9 8.9 %collective-permute-start.10 = (bf16[3,3,512,32]{2,3,1,0:T(8,128)(2,1)S(1)}, bf16[3,3,512,32]{2,3,1,0:T(8,128)(2,1)S(1)}, u32[]{:S(2)}, u32[]{:S(2)}) collective-permute-start(bf16[3,3,512,32]{2,3,1,0:T(8,128)(2,1)S(1)} %collective-permute-done.8), channel_id=1, source_target_pairs={{0,2},{2,4},{4,6},{6,8},{8,10},{10,12},{12,14},{14,16},{16,18},{18... | collective-permute-start | bytes 884744 | tf_op jit(solution)/shard_map/ppermute | solution.py:13
  58.0 8.9 %collective-permute-start.11 = (bf16[3,3,512,32]{2,3,1,0:T(8,128)(2,1)S(1)}, bf16[3,3,512,32]{2,3,1,0:T(8,128)(2,1)S(1)}, u32[]{:S(2)}, u32[]{:S(2)}) collective-permute-start(bf16[3,3,512,32]{2,3,1,0:T(8,128)(2,1)S(1)} %collective-permute-done.9), channel_id=1, source_target_pairs={{0,30},{2,0},{4,2},{6,4},{8,6},{10,8},{12,10},{14,12},{16,14},{18,... | collective-permute-start | bytes 884744 | tf_op jit(solution)/shard_map/ppermute | solution.py:16
  66.8 8.9 %collective-permute-start.12 = (bf16[3,3,512,32]{2,3,1,0:T(8,128)(2,1)S(1)}, bf16[3,3,512,32]{2,3,1,0:T(8,128)(2,1)S(1)}, u32[]{:S(2)}, u32[]{:S(2)}) collective-permute-start(bf16[3,3,512,32]{2,3,1,0:T(8,128)(2,1)S(1)} %collective-permute-done.10), channel_id=1, source_target_pairs={{0,2},{2,4},{4,6},{6,8},{8,10},{10,12},{12,14},{14,16},{16,18},{18... | collective-permute-start | bytes 884744 | tf_op jit(solution)/shard_map/ppermute | solution.py:13
  66.9 8.9 %collective-permute-start.13 = (bf16[3,3,512,32]{2,3,1,0:T(8,128)(2,1)S(1)}, bf16[3,3,512,32]{2,3,1,0:T(8,128)(2,1)S(1)}, u32[]{:S(2)}, u32[]{:S(2)}) collective-permute-start(bf16[3,3,512,32]{2,3,1,0:T(8,128)(2,1)S(1)} %collective-permute-done.11), channel_id=1, source_target_pairs={{0,30},{2,0},{4,2},{6,4},{8,6},{10,8},{12,10},{14,12},{16,14},{18,... | collective-permute-start | bytes 884744 | tf_op jit(solution)/shard_map/ppermute | solution.py:16
  75.8 8.8 %collective-permute-start.14 = (bf16[3,3,512,32]{2,3,1,0:T(8,128)(2,1)S(1)}, bf16[3,3,512,32]{2,3,1,0:T(8,128)(2,1)S(1)}, u32[]{:S(2)}, u32[]{:S(2)}) collective-permute-start(bf16[3,3,512,32]{2,3,1,0:T(8,128)(2,1)S(1)} %collective-permute-done.12), channel_id=1, source_target_pairs={{0,2},{2,4},{4,6},{6,8},{8,10},{10,12},{12,14},{14,16},{16,18},{18... | collective-permute-start | bytes 884744 | tf_op jit(solution)/shard_map/ppermute | solution.py:13
  75.9 8.8 %collective-permute-start.15 = (bf16[3,3,512,32]{2,3,1,0:T(8,128)(2,1)S(1)}, bf16[3,3,512,32]{2,3,1,0:T(8,128)(2,1)S(1)}, u32[]{:S(2)}, u32[]{:S(2)}) collective-permute-start(bf16[3,3,512,32]{2,3,1,0:T(8,128)(2,1)S(1)} %collective-permute-done.13), channel_id=1, source_target_pairs={{0,30},{2,0},{4,2},{6,4},{8,6},{10,8},{12,10},{14,12},{16,14},{18,... | collective-permute-start | bytes 884744 | tf_op jit(solution)/shard_map/ppermute | solution.py:16
  84.6 8.8 %collective-permute-start.16 = (bf16[3,3,512,32]{2,3,1,0:T(8,128)(2,1)S(1)}, bf16[3,3,512,32]{2,3,1,0:T(8,128)(2,1)S(1)}, u32[]{:S(2)}, u32[]{:S(2)}) collective-permute-start(bf16[3,3,512,32]{2,3,1,0:T(8,128)(2,1)S(1)} %collective-permute-done.14), channel_id=1, source_target_pairs={{0,2},{2,4},{4,6},{6,8},{8,10},{10,12},{12,14},{14,16},{16,18},{18... | collective-permute-start | bytes 884744 | tf_op jit(solution)/shard_map/ppermute | solution.py:13
  98.3 2.3 collective-permute-start.17
  100.6 2.4 copy-start.7
  101.6 124.0 %copy-start.6 = (f32[512]{0:T(512)S(1)}, f32[512]{0:T(512)}, u32[]{:S(2)}) copy-start(f32[512]{0:T(512)} %param.15) | copy-start | bytes 6148
  249.2 12.3 %copy-start.4 = (bf16[512,512]{1,0:T(8,128)(2,1)S(1)}, bf16[512,512]{1,0:T(8,128)(2,1)}, u32[]{:S(2)}) copy-start(bf16[512,512]{1,0:T(8,128)(2,1)} %param.17) | copy-start | bytes 1572868
  (3 other events, 5.8 us)
Sparse Core Ops, SparseCore 0:
  102.5 39.4 all-gather.2
